TPU v7x, 32 devices: a whole 2x2x4 slice. The times are simulated.
32 devices in a mesh: seq: 4 (over y, x), tp: 8 (over z, core).
Axes of the slice: x: 2, y: 2, z: 4, core: 2. Of those that a mesh axis runs over, the one named last changes fastest.
Arguments:
- tokens: bfloat16 [4096, 4096], P('seq'), may hold values from -32 to 32
- w_query: bfloat16 [4096, 2048], P(None, 'tp'), may hold values from -0.109375 to 0.109375
- w_key: bfloat16 [4096, 512], P(None, 'tp'), may hold values from -0.078125 to 0.078125
- w_value: bfloat16 [4096, 512], P(None, 'tp'), may hold values from -0.09375 to 0.09375
- w_out: bfloat16 [2048, 4096], P('tp'), may hold values from -0.1875 to 0.1875
- seg_ids: int32 [4096], replicated, may hold values from 0 to 31, as said below
- owner_counts: int32 [8], replicated, may hold values from 1 to 8, 32 in all
- centroids: bfloat16 [16384, 4096], P('seq', 'tp'), may hold values from -1.5 to 1.5
- pool_gain: float32 [4096], P('tp'), may hold values from 0.1 to 1.9
- assign: int32 [32], replicated, may hold values from 0 to 16383
Outputs:
- distances: float32 [64, 16384], P('tp', 'seq')
- updated: float32 [16384, 4096], P('seq', 'tp')
Inputs may be any that keep to these rules, and one draw needn't show every extreme that they name: `seg_ids`: ids never fall along the sequence; every id occurs; one instruction spans exactly 4065 tokens. `owner_counts`: the counts sum to 32; one owner holds exactly 8 rows.
All inputs are finite; a program needn't handle non-finite values.
Results may differ from a plain program's by a relative error of at most 0.0007.
Values may be sent and summed in bfloat16 or wider, within the bound.
No kernel may reach another device: no remote copies, remote signals or barrier semaphores. Data moves between devices by JAX's collectives and lax.ppermute only.
A program may use at most 192 MiB of HBM per device.

v0:
```python
import math
import jax
import jax.numpy as jnp
from jax import lax
from jax.sharding import PartitionSpec as P

HD = 128
WINDOW = 4096
QBLOCK = 512
rope_theta = 10000.0
norm_eps = 1e-06


def from_partner(x, axis, apart):
    return lax.ppermute(x, axis, [(i, i ^ 1 << apart) for i in range(lax.axis_size(axis))])


def from_behind(value, axis, steps):
    count = lax.axis_size(axis)
    leading, last = (max(0, -steps), min(count, count - steps))
    return lax.ppermute(value, axis, [(source, source + steps) for source in range(leading, last)])


def rotate_pairs(vectors, positions, first_pair, head_size):
    cols = vectors.shape[-1]
    pair_index = (first_pair + jnp.arange(cols // 2)).astype(jnp.float32)
    inverse = jnp.exp(-(2.0 * pair_index / head_size) * math.log(rope_theta))
    angles = positions.astype(jnp.float32)[:, None] * inverse[None, :]
    cosine = jnp.cos(angles)[:, None, :]
    sine = jnp.sin(angles)[:, None, :]
    paired = vectors.reshape(vectors.shape[:-1] + (cols // 2, 2))
    even_part = paired[..., 0]
    odd_part = paired[..., 1]
    turned = jnp.stack(
        [even_part * cosine - odd_part * sine, even_part * sine + odd_part * cosine], -1
    )
    return turned.reshape(vectors.shape)


def shards(
    tokens, w_query, w_key, w_value, w_out, seg_ids, owner_counts, centroids, pool_gain, assign
):
    tok_rows, model_width = tokens.shape
    half_cols = w_key.shape[1]
    heads_here = w_query.shape[1] // HD
    rank_seq = lax.axis_index("seq")
    rank_tp = lax.axis_index("tp")
    tp_total = lax.axis_size("tp")
    positions = rank_seq * tok_rows + jnp.arange(tok_rows, dtype=jnp.int32)
    queries = rotate_pairs(
        jnp.dot(tokens, w_query, preferred_element_type=jnp.float32).reshape(
            tok_rows, heads_here, HD
        ),
        positions,
        0,
        HD,
    ).astype(jnp.bfloat16)
    lower_first = rank_tp % 2 == 0
    key_half = jnp.dot(tokens, w_key, preferred_element_type=jnp.float32).reshape(
        tok_rows, 1, half_cols
    )
    key_half = rotate_pairs(key_half, positions, rank_tp % 2 * (half_cols // 2), HD).reshape(
        tok_rows, half_cols
    )
    value_half = jnp.dot(tokens, w_value, preferred_element_type=jnp.float32)
    own_pair = jnp.concatenate([key_half.astype(jnp.bfloat16), value_half.astype(jnp.bfloat16)], -1)
    partner = from_partner(own_pair, "tp", 0)
    front = jnp.where(lower_first, own_pair, partner)
    back = jnp.where(lower_first, partner, own_pair)
    key_rows = jnp.concatenate([front[:, :half_cols], back[:, :half_cols]], -1)
    value_rows = jnp.concatenate([front[:, half_cols:], back[:, half_cols:]], -1)
    kv_local = jnp.concatenate([key_rows, value_rows], -1)
    halo_shards = WINDOW // tok_rows
    reach = min(halo_shards, lax.axis_size("seq") - 1)
    pieces = [kv_local]
    for back_step in range(1, reach + 1):
        pieces.insert(0, from_behind(kv_local, "seq", back_step))
    if halo_shards > reach:
        pieces.insert(0, jnp.zeros(((halo_shards - reach) * tok_rows, 2 * HD), jnp.bfloat16))
    kv_window = jnp.concatenate(pieces, 0)
    pad_ids = jnp.concatenate([jnp.full((WINDOW,), -1, jnp.int32), seg_ids], 0)
    distance_grid = jnp.arange(QBLOCK)[:, None] + WINDOW - jnp.arange(WINDOW + QBLOCK)[None, :]
    outputs = []
    for block_index in range(tok_rows // QBLOCK):
        q_start = block_index * QBLOCK
        q_block = queries[q_start : q_start + QBLOCK]
        kv_block = kv_window[q_start : q_start + WINDOW + QBLOCK]
        q_ids = lax.dynamic_slice_in_dim(seg_ids, rank_seq * tok_rows + q_start, QBLOCK, 0)
        k_ids = lax.dynamic_slice_in_dim(pad_ids, rank_seq * tok_rows + q_start, WINDOW + QBLOCK, 0)
        allowed = (
            (distance_grid >= 0) & (distance_grid < WINDOW) & (q_ids[:, None] == k_ids[None, :])
        )
        scores = jnp.einsum(
            "qhd,kd->hqk", q_block, kv_block[:, :HD], preferred_element_type=jnp.float32
        ) * HD ** (-0.5)
        scores = jnp.where(allowed[None], scores, -1e30)
        highest = jnp.max(scores, axis=-1, keepdims=True)
        weights = jnp.exp(scores - highest)
        soft_weights = (weights / jnp.sum(weights, axis=-1, keepdims=True)).astype(jnp.bfloat16)
        head_out = jnp.einsum(
            "hqk,kd->qhd", soft_weights, kv_block[:, HD:], preferred_element_type=jnp.float32
        ).astype(jnp.bfloat16)
        outputs.append(head_out.reshape(QBLOCK, heads_here * HD))
    attention = jnp.concatenate(outputs, 0)
    seg_total = assign.shape[0]
    member = (
        lax.dynamic_slice_in_dim(seg_ids, rank_seq * tok_rows, tok_rows, 0)[:, None]
        == jnp.arange(seg_total, dtype=jnp.int32)[None, :]
    )
    member_float = member.astype(jnp.float32)
    member_half = member.astype(jnp.bfloat16)
    feat_cols = model_width // tp_total
    token_cols = lax.dynamic_slice_in_dim(tokens, rank_tp * feat_cols, feat_cols, 1)
    pooled_tokens = lax.dot_general(
        member_half, token_cols, (((0,), (0,)), ((), ())), preferred_element_type=jnp.float32
    )
    mixed_cols = lax.psum_scatter(
        lax.dot_general(
            w_out, attention, (((0,), (1,)), ((), ())), preferred_element_type=jnp.float32
        ),
        "tp",
        scatter_dimension=0,
        tiled=True,
    )
    pooled_mixed = lax.dot_general(
        member_float, mixed_cols, (((0,), (1,)), ((), ())), precision=lax.Precision.HIGHEST
    )
    seg_sums = lax.psum(pooled_tokens + pooled_mixed, "seq")
    counts = jnp.sum(
        (seg_ids[:, None] == jnp.arange(seg_total, dtype=jnp.int32)[None, :]).astype(jnp.float32),
        axis=0,
    )
    pooled = seg_sums / counts[:, None]
    square_sums = lax.psum(jnp.sum(pooled * pooled, axis=1), "tp")
    mean_square = square_sums / model_width
    embedding = pooled * lax.rsqrt(mean_square + norm_eps)[:, None] * pool_gain[None, :]
    cross_term = lax.dot_general(
        embedding.astype(jnp.bfloat16),
        centroids,
        (((1,), (1,)), ((), ())),
        preferred_element_type=jnp.float32,
    )
    cent_float = centroids.astype(jnp.float32)
    cent_norm = jnp.sum(cent_float * cent_float, axis=1)
    row_terms = (cent_norm[None, :] - 2.0 * cross_term) / model_width**0.5
    owners = owner_counts.shape[0]
    capacity = 2 * seg_total // owners
    starts = jnp.cumsum(owner_counts) - owner_counts
    slot_index = jnp.arange(capacity, dtype=jnp.int32)
    slot_rows = (starts[:, None] + slot_index[None, :]).reshape(-1)
    slot_valid = (slot_index[None, :] < owner_counts[:, None]).reshape(-1)
    selector = (
        (slot_rows[:, None] == jnp.arange(seg_total, dtype=jnp.int32)[None, :])
        & slot_valid[:, None]
    ).astype(jnp.float32)
    slot_terms = jnp.dot(selector, row_terms, precision=lax.Precision.HIGHEST)
    distances = lax.psum_scatter(slot_terms, "tp", scatter_dimension=0, tiled=True)
    cent_rows = centroids.shape[0]
    cent_ids = rank_seq * cent_rows + jnp.arange(cent_rows, dtype=jnp.int32)
    chosen = (assign[None, :] == cent_ids[:, None]).astype(jnp.float32)
    cent_sums = jnp.dot(chosen, embedding, precision=lax.Precision.HIGHEST)
    cent_counts = jnp.sum(chosen, axis=1)
    updated = (cent_float + cent_sums) / (1.0 + cent_counts)[:, None]
    return (distances, updated)


def solution(mesh):
    in_specs = (
        P("seq", None),
        P(None, "tp"),
        P(None, "tp"),
        P(None, "tp"),
        P("tp", None),
        P(),
        P(),
        P("seq", "tp"),
        P("tp"),
        P(),
    )
    out_specs = (P("tp", "seq"), P("seq", "tp"))
    return jax.shard_map(shards, mesh=mesh, in_specs=in_specs, out_specs=out_specs, check_vma=False)
```

profile of v0, /device:TPU:0, one launch (start us, length us, event | category | flops | bytes accessed | tf_op | source)
XLA Modules:
  0.0 416.3 jit_solution(12850956107057330214)
XLA Ops:
  7.3 6.3 %fusion.69 = f32[1024,64]{0,1:T(8,128)S(1)} fusion(bf16[1024,4096]{1,0:T(8,128)(2,1)} %param.10, bf16[4096,64]{0,1:T(8,128)(2,1)} %param.12), kind=kOutput, calls=%fused_computation.125 | convolution fusion | flops 536870912 | bytes 9175040 | tf_op jit(solution)/shard_map/dot_general | solution.py:59
  14.8 6.0 %convolution_convert_fusion = bf16[1024,64]{0,1:T(8,128)(2,1)S(1)} fusion(bf16[1024,4096]{1,0:T(8,128)(2,1)} %param.10, bf16[4096,64]{0,1:T(8,128)(2,1)S(1)} %copy-done.4), kind=kOutput, calls=%fused_computation.40 | convolution fusion | flops 536936448 | bytes 9043968 | tf_op jit(solution)/shard_map/dot_general | solution.py:65
  23.8 7.3 %fusion.70 = f32[1024,256]{0,1:T(8,128)} fusion(bf16[1024,4096]{1,0:T(8,128)(2,1)} %param.10, bf16[4096,256]{1,0:T(8,128)(2,1)} %param.11), kind=kOutput, calls=%fused_computation.126 | convolution fusion | flops 2147483648 | bytes 11534336 | tf_op jit(solution)/shard_map/dot_general | solution.py:51
  33.2 7.0 %compare_and_fusion.1 = (pred[512,4608]{0,1:T(8,128)(4,1)}, pred[512,4608]{0,1:T(8,128)(4,1)}) fusion(s32[512]{0:T(512)S(1)} %get-tuple-element.20, s32[512]{0:T(512)S(1)} %get-tuple-element.32, s32[4608]{0:T(1024)S(1)} %get-tuple-element.18, s32[4608]{0:T(1024)S(1)} %get-tuple-element.19, s32[512]{0:T(512)S(1)} %get-tuple-element.21), kind=kLoop, calls=%fused_computation.23 | loop fusion | flops 18874368 | bytes 4761600 | tf_op jit(solution)/shard_map/and | solution.py:91
  42.2 5.4 %collective-permute-start.1 = (bf16[1024,256]{0,1:T(8,128)(2,1)S(1)}, bf16[1024,256]{0,1:T(8,128)(2,1)S(1)}, u32[]{:S(2)}, u32[]{:S(2)}) collective-permute-start(bf16[1024,256]{0,1:T(8,128)(2,1)S(1)} %pad_maximum_fusion), channel_id=1, source_target_pairs={{0,24},{1,25},{2,26},{3,27},{4,28},{5,29},{6,30},{7,31}} | collective-permute-start | bytes 1572872 | tf_op jit(solution)/shard_map/ppermute | solution.py:21
  48.9 2.7 collective-permute-start.3
  53.2 6.6 %collective-permute-done.1 = bf16[1024,256]{0,1:T(8,128)(2,1)S(1)} collective-permute-done((bf16[1024,256]{0,1:T(8,128)(2,1)S(1)}, bf16[1024,256]{0,1:T(8,128)(2,1)S(1)}, u32[]{:S(2)}, u32[]{:S(2)}) %collective-permute-start.1) | collective-permute-done | bytes 524320 | tf_op jit(solution)/shard_map/ppermute | solution.py:21
  59.8 12.1 %collective-permute-done.2 = bf16[1024,256]{0,1:T(8,128)(2,1)S(1)} collective-permute-done((bf16[1024,256]{0,1:T(8,128)(2,1)S(1)}, bf16[1024,256]{0,1:T(8,128)(2,1)S(1)}, u32[]{:S(2)}, u32[]{:S(2)}) %collective-permute-start.2) | collective-permute-done | bytes 524320 | tf_op jit(solution)/shard_map/ppermute | solution.py:21
  72.1 8.3 %fusion.22 = f32[4608,512,2]{1,0,2:T(8,128)} fusion(bf16[5120,256]{0,1:T(8,128)(2,1)S(1)} %constant_dynamic-update-slice_fusion, bf16[512,2,128]{0,1,2:T(2,128)(2,1)S(1)} %bitcast.64), kind=kOutput, calls=%fused_computation.38 | convolution fusion | flops 1207959552 | bytes 20316160 | tf_op jit(solution)/shard_map/qhd,kd->hqk/dot_general | solution.py:93
  80.4 2.6 fusion.21
  83.0 21.7 %fusion.68 = (f32[2,512]{1,0:T(2,128)S(1)}, f32[2,512,4608]{1,2,0:T(8,128)}) fusion(f32[4608,512,2]{1,0,2:T(8,128)} %fusion.22, pred[512,4608]{0,1:T(8,128)(4,1)} %get-tuple-element.24), kind=kOutput, calls=%fused_computation.124 | output fusion | flops 28316160 | bytes 40112128 | tf_op jit(solution)/shard_map/sub | solution.py:98
  104.8 8.9 %fusion.20 = bf16[128,2,512]{2,0,1:T(8,128)(2,1)} fusion(f32[2,512,4608]{1,2,0:T(8,128)} %get-tuple-element.29, f32[2,512]{1,0:T(2,128)S(1)} %get-tuple-element.28, bf16[5120,256]{0,1:T(8,128)(2,1)} %copy-done.1), kind=kOutput, calls=%fused_computation.33 | convolution fusion | flops 1217527808 | bytes 20320256 | tf_op jit(solution)/shard_map/hqk,kd->qhd/dot_general | solution.py:100
  113.6 13.4 %fusion.67 = (f32[2,512]{1,0:T(2,128)S(1)}, f32[2,512,4608]{1,2,0:T(8,128)}) fusion(f32[4608,512,2]{1,0,2:T(8,128)S(1)} %fusion.21, pred[512,4608]{0,1:T(8,128)(4,1)} %get-tuple-element.25), kind=kOutput, calls=%fused_computation.123 | output fusion | flops 28316160 | bytes 40112128 | tf_op jit(solution)/shard_map/sub | solution.py:98
  127.0 8.2 %fusion.19 = bf16[128,2,512]{2,0,1:T(8,128)(2,1)S(1)} fusion(f32[2,512,4608]{1,2,0:T(8,128)} %get-tuple-element.27, f32[2,512]{1,0:T(2,128)S(1)} %get-tuple-element.26, bf16[5120,256]{0,1:T(8,128)(2,1)} %copy-done.1), kind=kOutput, calls=%fused_computation.32 | convolution fusion | flops 1217527808 | bytes 20320256 | tf_op jit(solution)/shard_map/hqk,kd->qhd/dot_general | solution.py:100
  135.2 8.1 %convolution_bitcast_fusion = f32[4096,1024]{0,1:T(8,128)} fusion(bf16[256,4096]{1,0:T(8,128)(2,1)S(1)} %copy-done, bf16[512,256]{0,1:T(8,128)(2,1)S(1)} %bitcast.66, bf16[512,256]{0,1:T(8,128)(2,1)S(1)} %bitcast.65), kind=kOutput, calls=%fused_computation.26 | convolution fusion | flops 2148532224 | bytes 19398656 | tf_op jit(solution)/shard_map/dot_general | solution.py:118
  144.5 3.1 fusion.15
  147.6 165.5 %reduce-scatter.3.cloned.1.call-done = f32[512,1024]{0,1:T(8,128)} async-done(((f32[4096,1024]{0,1:T(8,128)}), f32[512,1024]{0,1:T(8,128)}) %reduce-scatter.3.cloned.1.call-update) | async-done | bytes 2097168 | tf_op jit(solution)/shard_map/reduce_scatter | solution.py:117
  313.1 2.6 fusion.29
  315.6 2.3 convolution_add_fusion
  318.2 39.8 %all-reduce.3.cloned.1.call-done = f32[32,512]{1,0:T(8,128)} async-done(((f32[32,512]{1,0:T(8,128)}), f32[32,512]{1,0:T(8,128)}) %all-reduce.3.cloned.1.call-update) | async-done | bytes 65552 | tf_op jit(solution)/shard_map/psum | solution.py:128
  359.0 16.0 %psum.15 = f32[32]{0:T(128)S(1)} all-reduce(f32[32]{0:T(128)S(1)} %multiply_reduce_fusion), channel_id=1, replica_groups=mesh['seq'=4,'tp'=8] {'tp'}, use_global_device_ids=true, to_apply=%region_10.11 | all-reduce | flops 32 | bytes 256 | tf_op jit(solution)/shard_map/psum | solution.py:134
  375.0 3.6 fusion.18
  380.4 8.0 %fusion.16 = f32[4096,512]{1,0:T(8,128)} fusion(bf16[4096,512]{1,0:T(8,128)(2,1)} %param.17, f32[4096]{0:T(1024)S(1)} %broadcast_add_fusion, s32[4096]{0:T(1024)S(1)} %iota_add_fusion, s32[32]{0:T(128)S(1)} %copy-done.8, f32[512]{0:T(512)S(1)} %copy-done.7, f32[32]{0:T(128)S(1)} %add_rsqrt_fusion, f32[32,512]{1,0:T(8,128)} %all-reduce.3.cloned.1.call-done, ...), kind=kOutput, calls=%fused_computation.28 | convolution fusion | flops 811778048 | bytes 12683648 | tf_op jit(solution)/shard_map/dot_general | solution.py:161
  388.4 21.4 %reduce-scatter.5.cloned.1.call-done = f32[8,4096]{1,0:T(8,128)} async-done(((f32[64,4096]{1,0:T(8,128)}), f32[8,4096]{1,0:T(8,128)}) %reduce-scatter.5.cloned.1.call-update) | async-done | bytes 131088 | tf_op jit(solution)/shard_map/reduce_scatter | solution.py:157
  (69 shorter events, 15.4 us)
Async XLA Ops:
  7.2 128.0 %copy-start = (bf16[256,4096]{1,0:T(8,128)(2,1)S(1)}, bf16[256,4096]{1,0:T(8,128)(2,1)}, u32[]{:S(2)}) copy-start(bf16[256,4096]{1,0:T(8,128)(2,1)} %param.14) | copy-start | bytes 6291460
  7.2 7.6 %copy-start.4 = (bf16[4096,64]{0,1:T(8,128)(2,1)S(1)}, bf16[4096,64]{0,1:T(8,128)(2,1)}, u32[]{:S(2)}) copy-start(bf16[4096,64]{0,1:T(8,128)(2,1)} %param.13) | copy-start | bytes 1572868
  7.2 305.9 %reduce-scatter.3.cloned.1.call-start = ((), (), s32[]{:S(2)}) async-start(), calls=%async_computation.2 | async-start | bytes 18874368 | tf_op jit(solution)/shard_map/reduce_scatter | solution.py:117
  21.5 19.5 %collective-permute-start = (bf16[1024,128]{0,1:T(8,128)(2,1)}, bf16[1024,128]{0,1:T(8,128)(2,1)}, u32[]{:S(2)}, u32[]{:S(2)}) collective-permute-start(bf16[1024,128]{0,1:T(8,128)(2,1)} %pad_maximum_fusion.2), channel_id=1, source_target_pairs={{0,1},{1,0},{2,3},{3,2},{4,5},{5,4},{6,7},{7,6},{8,9},{9,8},{10,11... | collective-permute-start | bytes 786440 | tf_op jit(solution)/shard_map/ppermute | solution.py:15
  23.8 9.2 %copy-start.6 = (s32[4096]{0:T(1024)S(1)}, s32[4096]{0:T(1024)}, u32[]{:S(2)}) copy-start(s32[4096]{0:T(1024)} %param.15) | copy-start | bytes 49156
  33.0 18.6 %copy-start.2 = (f32[1024,64]{0,1:T(8,128)S(1)}, f32[1024,64]{0,1:T(8,128)}, u32[]{:S(2)}) copy-start(f32[1024,64]{0,1:T(8,128)} %get-tuple-element.22) | copy-start | bytes 786436
  33.0 18.6 %copy-start.3 = (f32[1024,64]{0,1:T(8,128)S(1)}, f32[1024,64]{0,1:T(8,128)}, u32[]{:S(2)}) copy-start(f32[1024,64]{0,1:T(8,128)} %get-tuple-element.23) | copy-start | bytes 786436
  42.2 17.6 %collective-permute-start.1 = (bf16[1024,256]{0,1:T(8,128)(2,1)S(1)}, bf16[1024,256]{0,1:T(8,128)(2,1)S(1)}, u32[]{:S(2)}, u32[]{:S(2)}) collective-permute-start(bf16[1024,256]{0,1:T(8,128)(2,1)S(1)} %pad_maximum_fusion), channel_id=1, source_target_pairs={{0,24},{1,25},{2,26},{3,27},{4,28},{5,29},{6,30},{7,31}} | collective-permute-start | bytes 1572872 | tf_op jit(solution)/shard_map/ppermute | solution.py:21
  47.6 24.4 %collective-permute-start.2 = (bf16[1024,256]{0,1:T(8,128)(2,1)S(1)}, bf16[1024,256]{0,1:T(8,128)(2,1)S(1)}, u32[]{:S(2)}, u32[]{:S(2)}) collective-permute-start(bf16[1024,256]{0,1:T(8,128)(2,1)S(1)} %pad_maximum_fusion), channel_id=1, source_target_pairs={{0,16},{8,24},{1,17},{9,25},{2,18},{10,26},{3,19},{11,27},{4,20},{... | collective-permute-start | bytes 1572872 | tf_op jit(solution)/shard_map/ppermute | solution.py:21
  48.9 23.1 %collective-permute-start.3 = (bf16[1024,256]{0,1:T(8,128)(2,1)S(1)}, bf16[1024,256]{0,1:T(8,128)(2,1)S(1)}, u32[]{:S(2)}, u32[]{:S(2)}) collective-permute-start(bf16[1024,256]{0,1:T(8,128)(2,1)S(1)} %pad_maximum_fusion), channel_id=1, source_target_pairs={{0,8},{8,16},{16,24},{1,9},{9,17},{17,25},{2,10},{10,18},{18,26},{... | collective-permute-start | bytes 1572872 | tf_op jit(solution)/shard_map/ppermute | solution.py:21
  72.1 8.3 %copy-start.1 = (bf16[5120,256]{0,1:T(8,128)(2,1)}, bf16[5120,256]{0,1:T(8,128)(2,1)S(1)}, u32[]{:S(2)}) copy-start(bf16[5120,256]{0,1:T(8,128)(2,1)S(1)} %constant_dynamic-update-slice_fusion) | copy-start | bytes 7864324
  127.0 8.2 %copy-start.5 = (bf16[128,2,512]{2,0,1:T(8,128)(2,1)S(1)}, bf16[128,2,512]{2,0,1:T(8,128)(2,1)}, u32[]{:S(2)}) copy-start(bf16[128,2,512]{2,0,1:T(8,128)(2,1)} %fusion.20) | copy-start | bytes 786436
  143.3 0.7 copy-start.9
  143.3 231.7 %copy-start.7 = (f32[512]{0:T(512)S(1)}, f32[512]{0:T(512)}, u32[]{:S(2)}) copy-start(f32[512]{0:T(512)} %param.18) | copy-start | bytes 6148
  143.4 236.9 %copy-start.8 = (s32[32]{0:T(128)S(1)}, s32[32]{0:T(128)}, u32[]{:S(2)}) copy-start(s32[32]{0:T(128)} %param.19) | copy-start | bytes 388
  143.4 214.6 %all-reduce.3.cloned.1.call-start = ((), (), s32[]{:S(2)}) async-start(), calls=%async_computation.3 | async-start | bytes 131072 | tf_op jit(solution)/shard_map/psum | solution.py:128
  318.0 91.7 %reduce-scatter.5.cloned.1.call-start = ((), (), s32[]{:S(2)}) async-start(), calls=%async_computation.4 | async-start | bytes 1179648 | tf_op jit(solution)/shard_map/reduce_scatter | solution.py:157
Sparse Core Ops, SparseCore 0:
  143.5 169.5 reduce-scatter.2
  318.1 39.8 all-reduce.2
  380.3 29.3 reduce-scatter.4
where the time goes:
time: 417 us; the launch traced here: 416 us
  waiting for transfers between devices  245 us (59%)
  matrix products  73.8 us (18%)
  other arithmetic  52.9 us (13%)
  blocking collectives  16 us (4%)
  between operations  14.1 us (3%)
  starting transfers between devices  9.94 us (2%)
  local copies, waits for them, and re-layouts  4.25 us (1%)
    reduce_scatter x1, waiting for transfers between devices, shards(): lax.psum_scatter(lax.dot_general(w_out, attention, (((0,), (1,)), ((), ()...  165 us
    psum x1, waiting for transfers between devices, shards(): seg_sums = lax.psum(pooled_tokens + pooled_mixed, 'seq')  39.8 us
    sub x2, other arithmetic, shards(): weights = jnp.exp(scores - highest)  35.1 us
    reduce_scatter x1, waiting for transfers between devices, shards(): lax.psum_scatter(slot_terms, 'tp', scatter_dimension=0, tiled=True)  21.4 us
    ppermute x3, waiting for transfers between devices, from_behind(): lax.ppermute(value, axis, [(source, source + steps) for source in range(l...  18.7 us
    dot_general x2, matrix products, shards(): jnp.einsum('hqk,kd->qhd', soft_weights, kv_block[:, HD:], preferred_eleme...  17 us
    psum x1, blocking collectives, shards(): square_sums = lax.psum(jnp.sum(pooled * pooled, axis=1), 'tp')  16 us
    dot_general x2, matrix products, shards(): jnp.einsum('qhd,kd->hqk', q_block, kv_block[:, :HD], preferred_element_ty...  11 us
  transfers between devices with their start and end apart: 7, of which 5 were waited for; matrix products, arithmetic and copies ran while one was open for 8% of the time, Pallas kernels for 0%

commit v1 on v0

--- a/solution.py
+++ b/solution.py
@@ -125,7 +125,9 @@
     pooled_mixed = lax.dot_general(
         member_float, mixed_cols, (((0,), (1,)), ((), ())), precision=lax.Precision.HIGHEST
     )
-    seg_sums = lax.psum(pooled_tokens + pooled_mixed, "seq")
+    part = pooled_tokens + pooled_mixed
+    blocks = lax.all_gather(part, "seq", axis=0, tiled=False)
+    seg_sums = blocks.sum(axis=0)
     counts = jnp.sum(
         (seg_ids[:, None] == jnp.arange(seg_total, dtype=jnp.int32)[None, :]).astype(jnp.float32),
         axis=0,

time: 417 us -> 382 us (0.916)
  waiting for transfers between devices: 245 us -> 205 us
  blocking collectives: 16 us -> 22.6 us
    psum x1 -> x0, waiting for transfers between devices: 39.8 us -> none  [shards(): seg_sums = lax.psum(pooled_tokens + pooled_mixed, 'seq')]
    all_gather x0 -> x1, blocking collectives: none -> 8.96 us  [shards(): blocks = lax.all_gather(part, 'seq', axis=0, tiled=False)]
  transfers between devices with their start and end apart: 7 -> 6, of which waited for: 5 -> 4; matrix products, arithmetic and copies ran while one was open for 8% -> 9% of each run, Pallas kernels for 0% -> 0%
where the time goes in v1:
time: 382 us
  waiting for transfers between devices  205 us (54%)
  matrix products  73.1 us (19%)
  other arithmetic  52.1 us (14%)
  blocking collectives  22.6 us (6%)
  between operations  14.4 us (4%)
  starting transfers between devices  9.9 us (3%)
  local copies, waits for them, and re-layouts  4.25 us (1%)
    reduce_scatter x1, waiting for transfers between devices, shards(): lax.psum_scatter(lax.dot_general(w_out, attention, (((0,), (1,)), ((), ()...  165 us
    sub x2, other arithmetic, shards(): weights = jnp.exp(scores - highest)  35.1 us
    reduce_scatter x1, waiting for transfers between devices, shards(): lax.psum_scatter(slot_terms, 'tp', scatter_dimension=0, tiled=True)  21.5 us
    ppermute x3, waiting for transfers between devices, from_behind(): lax.ppermute(value, axis, [(source, source + steps) for source in range(l...  18.7 us
    dot_general x2, matrix products, shards(): jnp.einsum('hqk,kd->qhd', soft_weights, kv_block[:, HD:], preferred_eleme...  17 us
    psum x1, blocking collectives, shards(): square_sums = lax.psum(jnp.sum(pooled * pooled, axis=1), 'tp')  13.6 us
    dot_general x2, matrix products, shards(): jnp.einsum('qhd,kd->hqk', q_block, kv_block[:, :HD], preferred_element_ty...  11 us
    ppermute x3, starting transfers between devices, from_behind(): lax.ppermute(value, axis, [(source, source + steps) for source in range(l...  9.37 us
  transfers between devices with their start and end apart: 6, of which 4 were waited for; matrix products, arithmetic and copies ran while one was open for 9% of the time, Pallas kernels for 0%

profile of v1, /device:TPU:0, one launch (start us, length us, event | category | flops | bytes accessed | tf_op | source)
XLA Modules:
  0.0 381.8 jit_solution(13312479673074202998)
XLA Ops:
  7.3 6.3 %fusion.69 = f32[1024,64]{0,1:T(8,128)S(1)} fusion(bf16[1024,4096]{1,0:T(8,128)(2,1)} %param.10, bf16[4096,64]{0,1:T(8,128)(2,1)} %param.12), kind=kOutput, calls=%fused_computation.125 | convolution fusion | flops 536870912 | bytes 9175040 | tf_op jit(solution)/shard_map/dot_general | solution.py:59
  14.8 6.0 %convolution_convert_fusion = bf16[1024,64]{0,1:T(8,128)(2,1)S(1)} fusion(bf16[1024,4096]{1,0:T(8,128)(2,1)} %param.10, bf16[4096,64]{0,1:T(8,128)(2,1)S(1)} %copy-done.4), kind=kOutput, calls=%fused_computation.40 | convolution fusion | flops 536936448 | bytes 9043968 | tf_op jit(solution)/shard_map/dot_general | solution.py:65
  23.8 7.3 %fusion.70 = f32[1024,256]{0,1:T(8,128)} fusion(bf16[1024,4096]{1,0:T(8,128)(2,1)} %param.10, bf16[4096,256]{1,0:T(8,128)(2,1)} %param.11), kind=kOutput, calls=%fused_computation.126 | convolution fusion | flops 2147483648 | bytes 11534336 | tf_op jit(solution)/shard_map/dot_general | solution.py:51
  31.1 1.8 reshape_reshape.8
  33.2 7.0 %compare_and_fusion.1 = (pred[512,4608]{0,1:T(8,128)(4,1)}, pred[512,4608]{0,1:T(8,128)(4,1)}) fusion(s32[512]{0:T(512)S(1)} %get-tuple-element.20, s32[512]{0:T(512)S(1)} %get-tuple-element.32, s32[4608]{0:T(1024)S(1)} %get-tuple-element.18, s32[4608]{0:T(1024)S(1)} %get-tuple-element.19, s32[512]{0:T(512)S(1)} %get-tuple-element.21), kind=kLoop, calls=%fused_computation.23 | loop fusion | flops 18874368 | bytes 4761600 | tf_op jit(solution)/shard_map/and | solution.py:91
  42.2 5.4 %collective-permute-start.1 = (bf16[1024,256]{0,1:T(8,128)(2,1)S(1)}, bf16[1024,256]{0,1:T(8,128)(2,1)S(1)}, u32[]{:S(2)}, u32[]{:S(2)}) collective-permute-start(bf16[1024,256]{0,1:T(8,128)(2,1)S(1)} %pad_maximum_fusion), channel_id=1, source_target_pairs={{0,24},{1,25},{2,26},{3,27},{4,28},{5,29},{6,30},{7,31}} | collective-permute-start | bytes 1572872 | tf_op jit(solution)/shard_map/ppermute | solution.py:21
  48.9 2.7 collective-permute-start.3
  53.2 6.6 %collective-permute-done.1 = bf16[1024,256]{0,1:T(8,128)(2,1)S(1)} collective-permute-done((bf16[1024,256]{0,1:T(8,128)(2,1)S(1)}, bf16[1024,256]{0,1:T(8,128)(2,1)S(1)}, u32[]{:S(2)}, u32[]{:S(2)}) %collective-permute-start.1) | collective-permute-done | bytes 524320 | tf_op jit(solution)/shard_map/ppermute | solution.py:21
  59.8 12.1 %collective-permute-done.2 = bf16[1024,256]{0,1:T(8,128)(2,1)S(1)} collective-permute-done((bf16[1024,256]{0,1:T(8,128)(2,1)S(1)}, bf16[1024,256]{0,1:T(8,128)(2,1)S(1)}, u32[]{:S(2)}, u32[]{:S(2)}) %collective-permute-start.2) | collective-permute-done | bytes 524320 | tf_op jit(solution)/shard_map/ppermute | solution.py:21
  72.1 8.3 %fusion.22 = f32[4608,512,2]{1,0,2:T(8,128)} fusion(bf16[5120,256]{0,1:T(8,128)(2,1)S(1)} %constant_dynamic-update-slice_fusion, bf16[512,2,128]{0,1,2:T(2,128)(2,1)S(1)} %bitcast.65), kind=kOutput, calls=%fused_computation.38 | convolution fusion | flops 1207959552 | bytes 20316160 | tf_op jit(solution)/shard_map/qhd,kd->hqk/dot_general | solution.py:93
  80.4 2.6 fusion.21
  83.0 21.7 %fusion.68 = (f32[2,512]{1,0:T(2,128)S(1)}, f32[2,512,4608]{1,2,0:T(8,128)}) fusion(f32[4608,512,2]{1,0,2:T(8,128)} %fusion.22, pred[512,4608]{0,1:T(8,128)(4,1)} %get-tuple-element.24), kind=kOutput, calls=%fused_computation.124 | output fusion | flops 28316160 | bytes 40112128 | tf_op jit(solution)/shard_map/sub | solution.py:98
  104.8 8.9 %fusion.20 = bf16[128,2,512]{2,0,1:T(8,128)(2,1)} fusion(f32[2,512,4608]{1,2,0:T(8,128)} %get-tuple-element.29, f32[2,512]{1,0:T(2,128)S(1)} %get-tuple-element.28, bf16[5120,256]{0,1:T(8,128)(2,1)} %copy-done.1), kind=kOutput, calls=%fused_computation.33 | convolution fusion | flops 1217527808 | bytes 20320256 | tf_op jit(solution)/shard_map/hqk,kd->qhd/dot_general | solution.py:100
  113.6 13.4 %fusion.67 = (f32[2,512]{1,0:T(2,128)S(1)}, f32[2,512,4608]{1,2,0:T(8,128)}) fusion(f32[4608,512,2]{1,0,2:T(8,128)S(1)} %fusion.21, pred[512,4608]{0,1:T(8,128)(4,1)} %get-tuple-element.25), kind=kOutput, calls=%fused_computation.123 | output fusion | flops 28316160 | bytes 40112128 | tf_op jit(solution)/shard_map/sub | solution.py:98
  127.0 8.2 %fusion.19 = bf16[128,2,512]{2,0,1:T(8,128)(2,1)S(1)} fusion(f32[2,512,4608]{1,2,0:T(8,128)} %get-tuple-element.27, f32[2,512]{1,0:T(2,128)S(1)} %get-tuple-element.26, bf16[5120,256]{0,1:T(8,128)(2,1)} %copy-done.1), kind=kOutput, calls=%fused_computation.32 | convolution fusion | flops 1217527808 | bytes 20320256 | tf_op jit(solution)/shard_map/hqk,kd->qhd/dot_general | solution.py:100
  135.2 8.1 %convolution_bitcast_fusion = f32[4096,1024]{0,1:T(8,128)} fusion(bf16[256,4096]{1,0:T(8,128)(2,1)S(1)} %copy-done, bf16[512,256]{0,1:T(8,128)(2,1)S(1)} %bitcast.68, bf16[512,256]{0,1:T(8,128)(2,1)S(1)} %bitcast.67), kind=kOutput, calls=%fused_computation.26 | convolution fusion | flops 2148532224 | bytes 19398656 | tf_op jit(solution)/shard_map/dot_general | solution.py:118
  144.7 3.1 fusion.15
  147.8 165.3 %reduce-scatter.3.cloned.1.call-done = f32[512,1024]{0,1:T(8,128)} async-done(((f32[4096,1024]{0,1:T(8,128)}), f32[512,1024]{0,1:T(8,128)}) %reduce-scatter.3.cloned.1.call-update) | async-done | bytes 2097168 | tf_op jit(solution)/shard_map/reduce_scatter | solution.py:117
  313.1 2.6 fusion.29
  317.3 9.0 %all-gather = f32[128,512]{1,0:T(8,128)S(1)} all-gather(f32[32,512]{1,0:T(8,128)S(1)} %convolution_add_fusion), channel_id=2, replica_groups=mesh['seq'=4,'tp'=8] {'seq'}, dimensions={0}, use_global_device_ids=true | all-gather | bytes 327680 | tf_op jit(solution)/shard_map/all_gather | solution.py:129
  326.5 13.6 %psum.7 = f32[32]{0:T(128)S(1)} all-reduce(f32[32]{0:T(128)S(1)} %multiply_reduce_fusion), channel_id=1, replica_groups=mesh['seq'=4,'tp'=8] {'tp'}, use_global_device_ids=true, to_apply=%region_10.11 | all-reduce | flops 32 | bytes 256 | tf_op jit(solution)/shard_map/psum | solution.py:136
  340.1 3.5 fusion.18
  345.5 8.0 %fusion.16 = f32[4096,512]{1,0:T(8,128)} fusion(bf16[4096,512]{1,0:T(8,128)(2,1)} %param.17, f32[4096]{0:T(1024)S(1)} %broadcast_add_fusion, s32[4096]{0:T(1024)S(1)} %iota_add_fusion, s32[32]{0:T(128)S(1)} %copy-done.8, f32[512]{0:T(512)S(1)} %copy-done.7, f32[32]{0:T(128)S(1)} %add_rsqrt_fusion, f32[32,512]{1,0:T(8,128)S(1)} %reduce_sum.66, ...), kind=kOutput, calls=%fused_computation.28 | convolution fusion | flops 811778048 | bytes 12683648 | tf_op jit(solution)/shard_map/dot_general | solution.py:163
  353.4 21.5 %reduce-scatter.5.cloned.1.call-done = f32[8,4096]{1,0:T(8,128)} async-done(((f32[64,4096]{1,0:T(8,128)}), f32[8,4096]{1,0:T(8,128)}) %reduce-scatter.5.cloned.1.call-update) | async-done | bytes 131088 | tf_op jit(solution)/shard_map/reduce_scatter | solution.py:159
  (68 shorter events, 14.4 us)
Async XLA Ops:
  7.2 128.0 %copy-start = (bf16[256,4096]{1,0:T(8,128)(2,1)S(1)}, bf16[256,4096]{1,0:T(8,128)(2,1)}, u32[]{:S(2)}) copy-start(bf16[256,4096]{1,0:T(8,128)(2,1)} %param.14) | copy-start | bytes 6291460
  7.2 7.6 %copy-start.4 = (bf16[4096,64]{0,1:T(8,128)(2,1)S(1)}, bf16[4096,64]{0,1:T(8,128)(2,1)}, u32[]{:S(2)}) copy-start(bf16[4096,64]{0,1:T(8,128)(2,1)} %param.13) | copy-start | bytes 1572868
  7.2 305.9 %reduce-scatter.3.cloned.1.call-start = ((), (), s32[]{:S(2)}) async-start(), calls=%async_computation.2 | async-start | bytes 18874368 | tf_op jit(solution)/shard_map/reduce_scatter | solution.py:117
  21.5 19.5 %collective-permute-start = (bf16[1024,128]{0,1:T(8,128)(2,1)}, bf16[1024,128]{0,1:T(8,128)(2,1)}, u32[]{:S(2)}, u32[]{:S(2)}) collective-permute-start(bf16[1024,128]{0,1:T(8,128)(2,1)} %pad_maximum_fusion.2), channel_id=1, source_target_pairs={{0,1},{1,0},{2,3},{3,2},{4,5},{5,4},{6,7},{7,6},{8,9},{9,8},{10,11... | collective-permute-start | bytes 786440 | tf_op jit(solution)/shard_map/ppermute | solution.py:15
  23.8 9.2 %copy-start.6 = (s32[4096]{0:T(1024)S(1)}, s32[4096]{0:T(1024)}, u32[]{:S(2)}) copy-start(s32[4096]{0:T(1024)} %param.15) | copy-start | bytes 49156
  33.0 18.6 %copy-start.2 = (f32[1024,64]{0,1:T(8,128)S(1)}, f32[1024,64]{0,1:T(8,128)}, u32[]{:S(2)}) copy-start(f32[1024,64]{0,1:T(8,128)} %get-tuple-element.22) | copy-start | bytes 786436
  33.0 18.6 %copy-start.3 = (f32[1024,64]{0,1:T(8,128)S(1)}, f32[1024,64]{0,1:T(8,128)}, u32[]{:S(2)}) copy-start(f32[1024,64]{0,1:T(8,128)} %get-tuple-element.23) | copy-start | bytes 786436
  42.2 17.6 %collective-permute-start.1 = (bf16[1024,256]{0,1:T(8,128)(2,1)S(1)}, bf16[1024,256]{0,1:T(8,128)(2,1)S(1)}, u32[]{:S(2)}, u32[]{:S(2)}) collective-permute-start(bf16[1024,256]{0,1:T(8,128)(2,1)S(1)} %pad_maximum_fusion), channel_id=1, source_target_pairs={{0,24},{1,25},{2,26},{3,27},{4,28},{5,29},{6,30},{7,31}} | collective-permute-start | bytes 1572872 | tf_op jit(solution)/shard_map/ppermute | solution.py:21
  47.6 24.4 %collective-permute-start.2 = (bf16[1024,256]{0,1:T(8,128)(2,1)S(1)}, bf16[1024,256]{0,1:T(8,128)(2,1)S(1)}, u32[]{:S(2)}, u32[]{:S(2)}) collective-permute-start(bf16[1024,256]{0,1:T(8,128)(2,1)S(1)} %pad_maximum_fusion), channel_id=1, source_target_pairs={{0,16},{8,24},{1,17},{9,25},{2,18},{10,26},{3,19},{11,27},{4,20},{... | collective-permute-start | bytes 1572872 | tf_op jit(solution)/shard_map/ppermute | solution.py:21
  48.9 23.1 %collective-permute-start.3 = (bf16[1024,256]{0,1:T(8,128)(2,1)S(1)}, bf16[1024,256]{0,1:T(8,128)(2,1)S(1)}, u32[]{:S(2)}, u32[]{:S(2)}) collective-permute-start(bf16[1024,256]{0,1:T(8,128)(2,1)S(1)} %pad_maximum_fusion), channel_id=1, source_target_pairs={{0,8},{8,16},{16,24},{1,9},{9,17},{17,25},{2,10},{10,18},{18,26},{... | collective-permute-start | bytes 1572872 | tf_op jit(solution)/shard_map/ppermute | solution.py:21
  72.1 8.3 %copy-start.1 = (bf16[5120,256]{0,1:T(8,128)(2,1)}, bf16[5120,256]{0,1:T(8,128)(2,1)S(1)}, u32[]{:S(2)}) copy-start(bf16[5120,256]{0,1:T(8,128)(2,1)S(1)} %constant_dynamic-update-slice_fusion) | copy-start | bytes 7864324
  127.0 8.2 %copy-start.5 = (bf16[128,2,512]{2,0,1:T(8,128)(2,1)S(1)}, bf16[128,2,512]{2,0,1:T(8,128)(2,1)}, u32[]{:S(2)}) copy-start(bf16[128,2,512]{2,0,1:T(8,128)(2,1)} %fusion.20) | copy-start | bytes 786436
  143.3 0.7 copy-start.9
  143.3 196.8 %copy-start.7 = (f32[512]{0:T(512)S(1)}, f32[512]{0:T(512)}, u32[]{:S(2)}) copy-start(f32[512]{0:T(512)} %param.18) | copy-start | bytes 6148
  143.4 202.0 %copy-start.8 = (s32[32]{0:T(128)S(1)}, s32[32]{0:T(128)}, u32[]{:S(2)}) copy-start(s32[32]{0:T(128)} %param.19) | copy-start | bytes 388
  143.4 231.6 %reduce-scatter.5.cloned.1.call-start = ((), (), s32[]{:S(2)}) async-start(), calls=%async_computation.3 | async-start | bytes 1179648 | tf_op jit(solution)/shard_map/reduce_scatter | solution.py:159
Sparse Core Ops, SparseCore 0:
  143.5 169.5 reduce-scatter.2
  345.4 29.4 reduce-scatter.4
